TPU v7x, 256 devices: a whole 4x4x8 slice. The times are simulated.
256 devices in a mesh: seq: 128 (over z, y, x), head: 2 (over core).
Axes of the slice: x: 4, y: 4, z: 8, core: 2. Of those that a mesh axis runs over, the one named last changes fastest.
Arguments:
- queries: bfloat16 [65536, 2048], P(('seq', 'head')), may hold values from -6 to 6
- key_rows: bfloat16 [65536, 2048], P(('seq', 'head')), may hold values from -6 to 6
- values: bfloat16 [65536, 2048], P(('seq', 'head')), may hold values from -6 to 6
- out_grad: bfloat16 [65536, 2048], P(('seq', 'head')), may hold values from -6 to 6
- level_weights: float32 [16, 11], replicated, may hold values from 0.2 to 1
Outputs:
- query_grad: bfloat16 [65536, 2048], P(('seq', 'head'))
- key_grad: bfloat16 [65536, 2048], P(('seq', 'head'))
- value_grad: bfloat16 [65536, 2048], P(('seq', 'head'))
All inputs are finite; a program needn't handle non-finite values.
Results may differ from a plain program's by a relative error of at most 0.003.
Values may be sent and summed in bfloat16 or wider, within the bound.
A program may use at most 128 MiB of HBM per device.

v0:
```python
import jax
import jax.numpy as jnp
from jax import lax
from jax.sharding import PartitionSpec as P

DH = 128
BLOCK = 128


def partner(array, axis, distance):
    return lax.ppermute(array, axis, [(i, i ^ 1 << distance) for i in range(lax.axis_size(axis))])


def fenwick_local(kv_blocks, qo_blocks, level_scale):
    block_count = kv_blocks.shape[0]
    inner_shape = kv_blocks.shape[1:]
    earlier = jnp.zeros_like(kv_blocks)
    later = jnp.zeros_like(qo_blocks)
    for level_index in range(1, block_count.bit_length()):
        half_span = 1 << level_index - 1
        group_count = block_count >> level_index
        weight = level_scale[:, level_index][:, None, None]
        kv_groups = kv_blocks.reshape((group_count, 2, half_span) + inner_shape)
        qo_groups = qo_blocks.reshape((group_count, 2, half_span) + inner_shape)
        lower_sum = jnp.sum(kv_groups[:, 0], axis=1) * weight
        upper_sum = jnp.sum(qo_groups[:, 1], axis=1) * weight
        zero_block = jnp.zeros_like(lower_sum)
        add_earlier = jnp.stack([zero_block, lower_sum], axis=1)[:, :, None]
        add_later = jnp.stack([upper_sum, zero_block], axis=1)[:, :, None]
        full_shape = (group_count, 2, half_span) + inner_shape
        earlier = earlier + jnp.broadcast_to(add_earlier, full_shape).reshape(kv_blocks.shape)
        later = later + jnp.broadcast_to(add_later, full_shape).reshape(qo_blocks.shape)
    return (earlier, later)


def cross_states(kv_total, qo_total, level_scale, local_levels, swapper, position, chain_len):
    earlier = jnp.zeros_like(kv_total)
    later = jnp.zeros_like(qo_total)
    group_kv = kv_total
    group_qo = qo_total
    for bit_index in range(chain_len.bit_length() - 1):
        other_kv, other_qo = swapper((group_kv, group_qo), bit_index)
        upper_half = (position // (1 << bit_index) % 2).astype(jnp.float32)
        weight = level_scale[:, local_levels + 1 + bit_index][:, None, None]
        earlier = earlier + upper_half * weight * other_kv
        later = later + (1.0 - upper_half) * weight * other_qo
        group_kv = group_kv + other_kv
        group_qo = group_qo + other_qo
    return (earlier, later)


def range_grads(
    query_rows, key_part, value_rows, grad_rows, level_scale, swapper, position, chain_len
):
    high = lax.Precision.HIGHEST
    token_count = query_rows.shape[0]
    head_count = query_rows.shape[1] // DH
    block_count = token_count // BLOCK
    shape_four = (block_count, BLOCK, head_count, DH)
    query_blk = query_rows.reshape(shape_four)
    key_blk = key_part.reshape(shape_four)
    value_blk = value_rows.reshape(shape_four)
    grad_blk = grad_rows.reshape(shape_four)
    rows = lax.broadcasted_iota(jnp.int32, (BLOCK, BLOCK), 0)
    cols = lax.broadcasted_iota(jnp.int32, (BLOCK, BLOCK), 1)
    causal_mask = (rows >= cols).astype(jnp.float32)
    first_weight = level_scale[:, 0][None, :, None, None]
    kv_blocks = jnp.einsum(
        "nshd,nshe->nhde", key_blk, value_blk, preferred_element_type=jnp.float32
    )
    qo_blocks = jnp.einsum(
        "nthd,nthe->nhde", query_blk, grad_blk, preferred_element_type=jnp.float32
    )
    local_levels = block_count.bit_length() - 1
    earlier_dev, later_dev = cross_states(
        jnp.sum(kv_blocks, axis=0),
        jnp.sum(qo_blocks, axis=0),
        level_scale,
        local_levels,
        swapper,
        position,
        chain_len,
    )
    scores = jnp.einsum("nthd,nshd->nhts", query_blk, key_blk, preferred_element_type=jnp.float32)
    weighted = (scores * causal_mask * first_weight).astype(jnp.bfloat16)
    grad_prob = jnp.einsum(
        "nthe,nshe->nhts", grad_blk, value_blk, preferred_element_type=jnp.float32
    )
    grad_score = (grad_prob * causal_mask * first_weight).astype(jnp.bfloat16)
    value_local = jnp.einsum(
        "nhts,nthe->nshe", weighted, grad_blk, preferred_element_type=jnp.float32
    )
    query_local = jnp.einsum(
        "nhts,nshd->nthd", grad_score, key_blk, preferred_element_type=jnp.float32
    )
    key_local = jnp.einsum(
        "nhts,nthd->nshd", grad_score, query_blk, preferred_element_type=jnp.float32
    )
    earlier_local, later_local = fenwick_local(kv_blocks, qo_blocks, level_scale)
    earlier = earlier_local + earlier_dev[None]
    later = later_local + later_dev[None]
    query_cross = jnp.einsum(
        "nthe,nhde->nthd", grad_blk, earlier, precision=high, preferred_element_type=jnp.float32
    )
    key_cross = jnp.einsum(
        "nshe,nhde->nshd", value_blk, later, precision=high, preferred_element_type=jnp.float32
    )
    value_cross = jnp.einsum(
        "nshd,nhde->nshe", key_blk, later, precision=high, preferred_element_type=jnp.float32
    )
    flat_shape = (token_count, head_count * DH)
    return (
        (query_local + query_cross).astype(jnp.bfloat16).reshape(flat_shape),
        (key_local + key_cross).astype(jnp.bfloat16).reshape(flat_shape),
        (value_local + value_cross).astype(jnp.bfloat16).reshape(flat_shape),
    )


def body(queries, key_rows, values, out_grad, level_weights):
    level_ids = jnp.arange(level_weights.shape[1], dtype=jnp.float32)
    level_scale = (
        level_weights
        * jnp.exp2((1.0 - level_ids) / 2.0)[None, :]
        / jnp.sqrt(jnp.float32(DH * BLOCK))
    )
    query_rows, key_part, value_rows, grad_rows = (
        lax.all_to_all(queries, "head", split_axis=1, concat_axis=0, tiled=True),
        lax.all_to_all(key_rows, "head", split_axis=1, concat_axis=0, tiled=True),
        lax.all_to_all(values, "head", split_axis=1, concat_axis=0, tiled=True),
        lax.all_to_all(out_grad, "head", split_axis=1, concat_axis=0, tiled=True),
    )
    head_count = level_scale.shape[0] // lax.axis_size("head")
    head_scale = lax.dynamic_slice_in_dim(
        level_scale, lax.axis_index("head") * head_count, head_count, 0
    )

    def swap_heads(states, bit_index):
        return partner(states, "seq", bit_index)

    query_part, key_grad_part, value_part = range_grads(
        query_rows,
        key_part,
        value_rows,
        grad_rows,
        head_scale,
        swap_heads,
        lax.axis_index("seq"),
        lax.axis_size("seq"),
    )
    return (
        lax.all_to_all(query_part, "head", split_axis=0, concat_axis=1, tiled=True),
        lax.all_to_all(key_grad_part, "head", split_axis=0, concat_axis=1, tiled=True),
        lax.all_to_all(value_part, "head", split_axis=0, concat_axis=1, tiled=True),
    )


def solution(mesh):
    return jax.shard_map(
        body,
        mesh=mesh,
        in_specs=(
            P(("seq", "head"), None),
            P(("seq", "head"), None),
            P(("seq", "head"), None),
            P(("seq", "head"), None),
            P(),
        ),
        out_specs=(P(("seq", "head"), None), P(("seq", "head"), None), P(("seq", "head"), None)),
        check_vma=False,
    )
```

profile of v0, /device:TPU:1, one launch (start us, length us, event | category | flops | bytes accessed | tf_op | source)
XLA Modules:
  0.0 267.1 jit_solution(1590416939446828161)
XLA Ops:
  0.6 2.4 copy.180
  3.0 6.8 %all-to-all-start = ((bf16[256,2,1024]{2,0,1:T(8,128)(2,1)}), bf16[256,2,1024]{2,0,1:T(8,128)(2,1)S(1)}, u32[]{:S(2)}, u32[]{:S(2)}) async-start(bf16[256,2,1024]{2,0,1:T(8,128)(2,1)} %bitcast.96), calls=%async_computation | async-start | bytes 2097152 | tf_op jit(solution)/shard_map/all_to_all | solution.py:130
  9.8 1.1 copy.177
  11.6 3.9 %all-to-all-start.4 = ((bf16[256,2,1024]{2,0,1:T(8,128)(2,1)}), bf16[256,2,1024]{2,0,1:T(8,128)(2,1)S(1)}, u32[]{:S(2)}, u32[]{:S(2)}) async-start(bf16[256,2,1024]{2,0,1:T(8,128)(2,1)} %bitcast.93), calls=%async_computation.4 | async-start | bytes 2097152 | tf_op jit(solution)/shard_map/all_to_all | solution.py:127
  15.8 1.5 all-to-all-done.4
  17.5 2.7 %fusion.31 = (f32[8,128,128]{2,1,0:T(8,128)}, f32[4,8,128,128]{3,2,1,0:T(8,128)}) fusion(bf16[4,128,8,128]{3,2,1,0:T(8,128)(2,1)S(1)} %bitcast.101, bf16[4,128,8,128]{3,2,1,0:T(8,128)(2,1)S(1)} %bitcast.105), kind=kOutput, calls=%fused_computation.72 | convolution fusion | flops 134610944 | bytes 4718592 | tf_op jit(solution)/shard_map/nthd,nthe->nhde/dot_general | solution.py:71
  20.2 1.1 copy.178
  21.3 3.9 %all-to-all-start.2 = ((bf16[256,2,1024]{2,0,1:T(8,128)(2,1)}), bf16[256,2,1024]{2,0,1:T(8,128)(2,1)S(1)}, u32[]{:S(2)}, u32[]{:S(2)}) async-start(bf16[256,2,1024]{2,0,1:T(8,128)(2,1)} %bitcast.119), calls=%async_computation.2 | async-start | bytes 2097152 | tf_op jit(solution)/shard_map/all_to_all | solution.py:128
  25.2 2.3 copy.179
  27.5 4.4 %all-to-all-start.1 = ((bf16[256,2,1024]{2,0,1:T(8,128)(2,1)}), bf16[256,2,1024]{2,0,1:T(8,128)(2,1)}, u32[]{:S(2)}, u32[]{:S(2)}) async-start(bf16[256,2,1024]{2,0,1:T(8,128)(2,1)} %bitcast.118), calls=%async_computation.1 | async-start | bytes 2097152 | tf_op jit(solution)/shard_map/all_to_all | solution.py:129
  32.0 1.5 copy.133
  33.8 1.5 copy.132
  35.3 2.6 fusion.30
  38.0 1.7 collective-permute-start
  39.7 2.0 add.176
  41.8 1.0 collective-permute-start.8
  42.8 1.5 slice_reduce_fusion
  44.3 7.7 %collective-permute-done = f32[8,128,128]{2,1,0:T(8,128)} collective-permute-done((f32[8,128,128]{2,1,0:T(8,128)}, f32[8,128,128]{2,1,0:T(8,128)}, u32[]{:S(2)}, u32[]{:S(2)}) %collective-permute-start) | collective-permute-done | bytes 524320 | tf_op jit(solution)/shard_map/ppermute | solution.py:11
  52.0 1.3 add.154
  53.3 1.7 collective-permute-start.1
  55.0 9.0 %collective-permute-done.8 = f32[8,128,128]{2,1,0:T(8,128)} collective-permute-done((f32[8,128,128]{2,1,0:T(8,128)}, f32[8,128,128]{2,1,0:T(8,128)}, u32[]{:S(2)}, u32[]{:S(2)}) %collective-permute-start.8) | collective-permute-done | bytes 524320 | tf_op jit(solution)/shard_map/ppermute | solution.py:11
  63.9 1.3 add.178
  65.2 1.4 collective-permute-start.9
  67.2 7.9 %collective-permute-done.1 = f32[8,128,128]{2,1,0:T(8,128)S(1)} collective-permute-done((f32[8,128,128]{2,1,0:T(8,128)S(1)}, f32[8,128,128]{2,1,0:T(8,128)S(1)}, u32[]{:S(2)}, u32[]{:S(2)}) %collective-permute-start.1) | collective-permute-done | bytes 524320 | tf_op jit(solution)/shard_map/ppermute | solution.py:11
  75.2 1.4 collective-permute-start.2
  76.8 3.0 %collective-permute-start.10 = (f32[8,128,128]{2,1,0:T(8,128)S(1)}, f32[8,128,128]{2,1,0:T(8,128)S(1)}, u32[]{:S(2)}, u32[]{:S(2)}) collective-permute-start(f32[8,128,128]{2,1,0:T(8,128)S(1)} %add.180), channel_id=1, source_target_pairs={{0,16},{2,18},{4,20},{6,22},{8,24},{10,26},{12,28},{14,30},{16,0},... | collective-permute-start | bytes 1572872 | tf_op jit(solution)/shard_map/ppermute | solution.py:11
  80.1 1.1 pad_bitcast_fusion
  81.2 1.2 fusion.4
  82.4 6.9 %collective-permute-done.2 = f32[8,128,128]{2,1,0:T(8,128)S(1)} collective-permute-done((f32[8,128,128]{2,1,0:T(8,128)S(1)}, f32[8,128,128]{2,1,0:T(8,128)S(1)}, u32[]{:S(2)}, u32[]{:S(2)}) %collective-permute-start.2) | collective-permute-done | bytes 524320 | tf_op jit(solution)/shard_map/ppermute | solution.py:11
  91.0 2.9 %collective-permute-start.3 = (f32[8,128,128]{2,1,0:T(8,128)}, f32[8,128,128]{2,1,0:T(8,128)}, u32[]{:S(2)}, u32[]{:S(2)}) collective-permute-start(f32[8,128,128]{2,1,0:T(8,128)} %add.160), channel_id=1, source_target_pairs={{0,16},{2,18},{4,20},{6,22},{8,24},{10,26},{12,28},{14,30},{16,0},... | collective-permute-start | bytes 1572872 | tf_op jit(solution)/shard_map/ppermute | solution.py:11
  93.9 9.1 %collective-permute-done.10 = f32[8,128,128]{2,1,0:T(8,128)S(1)} collective-permute-done((f32[8,128,128]{2,1,0:T(8,128)S(1)}, f32[8,128,128]{2,1,0:T(8,128)S(1)}, u32[]{:S(2)}, u32[]{:S(2)}) %collective-permute-start.10) | collective-permute-done | bytes 524320 | tf_op jit(solution)/shard_map/ppermute | solution.py:11
  104.6 1.6 collective-permute-start.11
  106.2 1.5 pad_add_fusion
  107.7 2.9 %copy.102 = f32[2,2,8,128,128]{3,4,2,1,0:T(8,128)} copy(f32[2,2,8,128,128]{4,3,2,0,1:T(8,128)} %pad_add_fusion) | data formatting | bytes 4194304 | tf_op jit(solution)/shard_map/add | solution.py:32
  110.7 1.7 pad_add_fusion.1
  112.4 1.5 copy.91
  114.3 1.3 add.163
  115.6 1.7 collective-permute-start.4
  117.3 1.3 add.184
  118.5 3.2 %collective-permute-start.12 = (f32[8,128,128]{2,1,0:T(8,128)S(1)}, f32[8,128,128]{2,1,0:T(8,128)S(1)}, u32[]{:S(2)}, u32[]{:S(2)}) collective-permute-start(f32[8,128,128]{2,1,0:T(8,128)S(1)} %add.184), channel_id=1, source_target_pairs={{0,64},{2,66},{4,68},{6,70},{8,72},{10,74},{12,76},{14,78},{16,80}... | collective-permute-start | bytes 1572872 | tf_op jit(solution)/shard_map/ppermute | solution.py:11
  122.7 1.9 fusion.12
  124.5 12.8 %collective-permute-done.4 = f32[8,128,128]{2,1,0:T(8,128)S(1)} collective-permute-done((f32[8,128,128]{2,1,0:T(8,128)S(1)}, f32[8,128,128]{2,1,0:T(8,128)S(1)}, u32[]{:S(2)}, u32[]{:S(2)}) %collective-permute-start.4) | collective-permute-done | bytes 524320 | tf_op jit(solution)/shard_map/ppermute | solution.py:11
  139.0 1.7 collective-permute-start.5
  142.3 5.3 %collective-permute-start.13 = (f32[8,128,128]{2,1,0:T(8,128)}, f32[8,128,128]{2,1,0:T(8,128)}, u32[]{:S(2)}, u32[]{:S(2)}) collective-permute-start(f32[8,128,128]{2,1,0:T(8,128)} %add.186), channel_id=1, source_target_pairs={{0,128},{2,130},{4,132},{6,134},{8,136},{10,138},{12,140},{14,142}... | collective-permute-start | bytes 1572872 | tf_op jit(solution)/shard_map/ppermute | solution.py:11
  147.7 1.7 fusion.22
  149.4 2.6 fusion.3
  151.9 26.1 %collective-permute-done.5 = f32[8,128,128]{2,1,0:T(8,128)} collective-permute-done((f32[8,128,128]{2,1,0:T(8,128)}, f32[8,128,128]{2,1,0:T(8,128)}, u32[]{:S(2)}, u32[]{:S(2)}) %collective-permute-start.5) | collective-permute-done | bytes 524320 | tf_op jit(solution)/shard_map/ppermute | solution.py:11
  178.1 2.1 add.169
  180.2 13.8 %collective-permute-start.6 = (f32[8,128,128]{2,1,0:T(8,128)}, f32[8,128,128]{2,1,0:T(8,128)}, u32[]{:S(2)}, u32[]{:S(2)}) collective-permute-start(f32[8,128,128]{2,1,0:T(8,128)} %add.169), channel_id=1, source_target_pairs={{0,128},{2,130},{4,132},{6,134},{8,136},{10,138},{12,140},{14,142}... | collective-permute-start | bytes 1572872 | tf_op jit(solution)/shard_map/ppermute | solution.py:11
  194.0 2.3 multiply_add_fusion
  196.3 1.0 copy.103
  197.3 2.1 bitcast_add_fusion.2
  199.7 2.3 fusion
  202.7 1.3 all_to_all.110
  204.0 33.7 %all_to_all.121 = bf16[2,256,1024]{2,1,0:T(8,128)(2,1)} all-to-all(bf16[2,256,1024]{2,1,0:T(8,128)(2,1)} %all_to_all.110), channel_id=1, replica_groups=mesh['seq'=128,'head'=2] {'head'}, dimensions={0} | all-to-all | bytes 2097152 | tf_op jit(solution)/shard_map/all_to_all | solution.py:153
  237.7 2.3 copy.116
  240.0 2.3 copy.119
  242.3 2.9 %fusion.1 = bf16[4,128,8,128]{3,1,2,0:T(8,128)(2,1)S(1)} fusion(f32[4,8,128,128]{3,2,1,0:T(8,128)} %fusion.12, f32[4,8,128,128]{2,3,1,0:T(8,128)S(1)} %bitcast_add_fusion.2, bf16[4,128,8,128]{3,2,1,0:T(8,128)(2,1)S(1)} %bitcast.110), kind=kOutput, calls=%fused_computation.3 | convolution fusion | flops 806354944 | bytes 6291456 | tf_op jit(solution)/shard_map/nshe,nhde->nshd/dot_general | solution.py:105
  246.4 4.7 %all_to_all.122 = bf16[2,256,1024]{2,1,0:T(8,128)(2,1)S(1)} all-to-all(bf16[2,256,1024]{2,1,0:T(8,128)(2,1)S(1)} %all_to_all.106), channel_id=1, replica_groups=mesh['seq'=128,'head'=2] {'head'}, dimensions={0} | all-to-all | bytes 2097152 | tf_op jit(solution)/shard_map/all_to_all | solution.py:152
  251.6 1.4 copy.118
  253.1 2.0 multiply_add_fusion.1
  257.2 2.3 fusion.2
  260.7 4.5 %all_to_all.123 = bf16[2,256,1024]{2,1,0:T(8,128)(2,1)S(1)} all-to-all(bf16[2,256,1024]{2,1,0:T(8,128)(2,1)S(1)} %all_to_all.99), channel_id=1, replica_groups=mesh['seq'=128,'head'=2] {'head'}, dimensions={0} | all-to-all | bytes 2097152 | tf_op jit(solution)/shard_map/all_to_all | solution.py:151
  265.7 1.4 copy.117
  (81 shorter events, 17.2 us)
Async XLA Ops:
  0.6 9.2 %copy-start.20 = (bf16[256,2048]{1,0:T(8,128)(2,1)S(1)}, bf16[256,2048]{1,0:T(8,128)(2,1)}, u32[]{:S(2)}) copy-start(bf16[256,2048]{1,0:T(8,128)(2,1)} %param.5) | copy-start | bytes 3145732
  3.0 8.6 %all-to-all-start = ((bf16[256,2,1024]{2,0,1:T(8,128)(2,1)}), bf16[256,2,1024]{2,0,1:T(8,128)(2,1)S(1)}, u32[]{:S(2)}, u32[]{:S(2)}) async-start(bf16[256,2,1024]{2,0,1:T(8,128)(2,1)} %bitcast.96), calls=%async_computation | async-start | bytes 2097152 | tf_op jit(solution)/shard_map/all_to_all | solution.py:130
  11.6 5.7 %all-to-all-start.4 = ((bf16[256,2,1024]{2,0,1:T(8,128)(2,1)}), bf16[256,2,1024]{2,0,1:T(8,128)(2,1)S(1)}, u32[]{:S(2)}, u32[]{:S(2)}) async-start(bf16[256,2,1024]{2,0,1:T(8,128)(2,1)} %bitcast.93), calls=%async_computation.4 | async-start | bytes 2097152 | tf_op jit(solution)/shard_map/all_to_all | solution.py:127
  15.8 133.6 %copy-start = (bf16[64,8,8,128]{3,2,1,0:T(8,128)(2,1)}, bf16[64,8,8,128]{3,2,1,0:T(8,128)(2,1)S(1)}, u32[]{:S(2)}) copy-start(bf16[64,8,8,128]{3,2,1,0:T(8,128)(2,1)S(1)} %copy.131) | copy-start | bytes 3145732
  17.5 2.7 %copy-start.21 = (bf16[256,2048]{1,0:T(8,128)(2,1)S(1)}, bf16[256,2048]{1,0:T(8,128)(2,1)}, u32[]{:S(2)}) copy-start(bf16[256,2048]{1,0:T(8,128)(2,1)} %param.6) | copy-start | bytes 3145732
  20.2 19.5 %collective-permute-start.7 = (f32[8,128,128]{2,1,0:T(8,128)}, f32[8,128,128]{2,1,0:T(8,128)}, u32[]{:S(2)}, u32[]{:S(2)}) collective-permute-start(f32[8,128,128]{2,1,0:T(8,128)} %get-tuple-element.32), channel_id=1, source_target_pairs={{0,2},{2,0},{4,6},{6,4},{8,10},{10,8},{12,14},{14,12},{16,18},{18,... | collective-permute-start | bytes 1572872 | tf_op jit(solution)/shard_map/ppermute | solution.py:11
  21.3 6.2 %all-to-all-start.2 = ((bf16[256,2,1024]{2,0,1:T(8,128)(2,1)}), bf16[256,2,1024]{2,0,1:T(8,128)(2,1)S(1)}, u32[]{:S(2)}, u32[]{:S(2)}) async-start(bf16[256,2,1024]{2,0,1:T(8,128)(2,1)} %bitcast.119), calls=%async_computation.2 | async-start | bytes 2097152 | tf_op jit(solution)/shard_map/all_to_all | solution.py:128
  27.5 4.4 %copy-start.10 = (bf16[256,2,1024]{2,0,1:T(8,128)(2,1)}, bf16[256,2,1024]{2,0,1:T(8,128)(2,1)S(1)}, u32[]{:S(2)}) copy-start(bf16[256,2,1024]{2,0,1:T(8,128)(2,1)S(1)} %all-to-all-done.2) | copy-start | bytes 3145732
  27.5 6.3 %all-to-all-start.1 = ((bf16[256,2,1024]{2,0,1:T(8,128)(2,1)}), bf16[256,2,1024]{2,0,1:T(8,128)(2,1)}, u32[]{:S(2)}, u32[]{:S(2)}) async-start(bf16[256,2,1024]{2,0,1:T(8,128)(2,1)} %bitcast.118), calls=%async_computation.1 | async-start | bytes 2097152 | tf_op jit(solution)/shard_map/all_to_all | solution.py:129
  35.3 2.7 copy-start.2
  38.0 6.3 %copy-start.22 = (f32[16,11]{1,0:T(8,128)S(1)}, f32[16,11]{1,0:T(8,128)}, u32[]{:S(2)}) copy-start(f32[16,11]{1,0:T(8,128)} %param.9) | copy-start | bytes 2116
  38.0 14.1 %collective-permute-start = (f32[8,128,128]{2,1,0:T(8,128)}, f32[8,128,128]{2,1,0:T(8,128)}, u32[]{:S(2)}, u32[]{:S(2)}) collective-permute-start(f32[8,128,128]{2,1,0:T(8,128)} %get-tuple-element.30), channel_id=1, source_target_pairs={{0,2},{2,0},{4,6},{6,4},{8,10},{10,8},{12,14},{14,12},{16,18},{18,... | collective-permute-start | bytes 1572872 | tf_op jit(solution)/shard_map/ppermute | solution.py:11
  41.8 22.2 %collective-permute-start.8 = (f32[8,128,128]{2,1,0:T(8,128)}, f32[8,128,128]{2,1,0:T(8,128)}, u32[]{:S(2)}, u32[]{:S(2)}) collective-permute-start(f32[8,128,128]{2,1,0:T(8,128)} %add.176), channel_id=1, source_target_pairs={{0,4},{2,6},{4,0},{6,2},{8,12},{10,14},{12,8},{14,10},{16,20},{18,... | collective-permute-start | bytes 1572872 | tf_op jit(solution)/shard_map/ppermute | solution.py:11
  42.8 24.1 %copy-start.8 = (f32[4,8,128,128]{3,2,1,0:T(8,128)S(1)}, f32[4,8,128,128]{3,2,1,0:T(8,128)}, u32[]{:S(2)}) copy-start(f32[4,8,128,128]{3,2,1,0:T(8,128)} %get-tuple-element.31) | copy-start | bytes 6291460
  53.3 21.8 %collective-permute-start.1 = (f32[8,128,128]{2,1,0:T(8,128)S(1)}, f32[8,128,128]{2,1,0:T(8,128)S(1)}, u32[]{:S(2)}, u32[]{:S(2)}) collective-permute-start(f32[8,128,128]{2,1,0:T(8,128)S(1)} %add.154), channel_id=1, source_target_pairs={{0,4},{2,6},{4,0},{6,2},{8,12},{10,14},{12,8},{14,10},{16,20},{18,... | collective-permute-start | bytes 1572872 | tf_op jit(solution)/shard_map/ppermute | solution.py:11
  65.2 11.5 %collective-permute-start.9 = (f32[8,128,128]{2,1,0:T(8,128)S(1)}, f32[8,128,128]{2,1,0:T(8,128)S(1)}, u32[]{:S(2)}, u32[]{:S(2)}) collective-permute-start(f32[8,128,128]{2,1,0:T(8,128)S(1)} %add.178), channel_id=1, source_target_pairs={{0,8},{2,10},{4,12},{6,14},{8,0},{10,2},{12,4},{14,6},{16,24},{18,... | collective-permute-start | bytes 1572872 | tf_op jit(solution)/shard_map/ppermute | solution.py:11
  75.1 6.1 %copy-start.11 = (f32[8,128,128]{2,1,0:T(8,128)}, f32[8,128,128]{2,1,0:T(8,128)S(1)}, u32[]{:S(2)}) copy-start(f32[8,128,128]{2,1,0:T(8,128)S(1)} %collective-permute-done.1) | copy-start | bytes 1572868
  75.2 6.0 %copy-start.7 = (f32[4,8,128,128]{3,2,1,0:T(8,128)S(1)}, f32[4,8,128,128]{3,2,1,0:T(8,128)}, u32[]{:S(2)}) copy-start(f32[4,8,128,128]{3,2,1,0:T(8,128)} %get-tuple-element.33) | copy-start | bytes 6291460
  75.2 14.1 %collective-permute-start.2 = (f32[8,128,128]{2,1,0:T(8,128)S(1)}, f32[8,128,128]{2,1,0:T(8,128)S(1)}, u32[]{:S(2)}, u32[]{:S(2)}) collective-permute-start(f32[8,128,128]{2,1,0:T(8,128)S(1)} %add.157), channel_id=1, source_target_pairs={{0,8},{2,10},{4,12},{6,14},{8,0},{10,2},{12,4},{14,6},{16,24},{18,... | collective-permute-start | bytes 1572872 | tf_op jit(solution)/shard_map/ppermute | solution.py:11
  76.7 3.4 %copy-start.15 = (f32[8,128,128]{2,1,0:T(8,128)}, f32[8,128,128]{2,1,0:T(8,128)S(1)}, u32[]{:S(2)}) copy-start(f32[8,128,128]{2,1,0:T(8,128)S(1)} %collective-permute-done.9) | copy-start | bytes 1572868
  76.8 26.2 %collective-permute-start.10 = (f32[8,128,128]{2,1,0:T(8,128)S(1)}, f32[8,128,128]{2,1,0:T(8,128)S(1)}, u32[]{:S(2)}, u32[]{:S(2)}) collective-permute-start(f32[8,128,128]{2,1,0:T(8,128)S(1)} %add.180), channel_id=1, source_target_pairs={{0,16},{2,18},{4,20},{6,22},{8,24},{10,26},{12,28},{14,30},{16,0},... | collective-permute-start | bytes 1572872 | tf_op jit(solution)/shard_map/ppermute | solution.py:11
  89.3 0.8 copy-start.13
  91.0 23.3 %collective-permute-start.3 = (f32[8,128,128]{2,1,0:T(8,128)}, f32[8,128,128]{2,1,0:T(8,128)}, u32[]{:S(2)}, u32[]{:S(2)}) collective-permute-start(f32[8,128,128]{2,1,0:T(8,128)} %add.160), channel_id=1, source_target_pairs={{0,16},{2,18},{4,20},{6,22},{8,24},{10,26},{12,28},{14,30},{16,0},... | collective-permute-start | bytes 1572872 | tf_op jit(solution)/shard_map/ppermute | solution.py:11
  103.0 0.8 copy-start.16
  104.6 12.7 %collective-permute-start.11 = (f32[8,128,128]{2,1,0:T(8,128)}, f32[8,128,128]{2,1,0:T(8,128)}, u32[]{:S(2)}, u32[]{:S(2)}) collective-permute-start(f32[8,128,128]{2,1,0:T(8,128)} %add.182), channel_id=1, source_target_pairs={{0,32},{2,34},{4,36},{6,38},{8,40},{10,42},{12,44},{14,46},{16,48}... | collective-permute-start | bytes 1572872 | tf_op jit(solution)/shard_map/ppermute | solution.py:11
  113.9 7.9 %copy-start.3 = (bf16[64,8,8,128]{3,2,1,0:T(8,128)(2,1)S(1)}, bf16[64,8,8,128]{3,2,1,0:T(8,128)(2,1)}, u32[]{:S(2)}) copy-start(bf16[64,8,8,128]{3,2,1,0:T(8,128)(2,1)} %copy-done.2) | copy-start | bytes 3145732
  115.6 21.8 %collective-permute-start.4 = (f32[8,128,128]{2,1,0:T(8,128)S(1)}, f32[8,128,128]{2,1,0:T(8,128)S(1)}, u32[]{:S(2)}, u32[]{:S(2)}) collective-permute-start(f32[8,128,128]{2,1,0:T(8,128)S(1)} %add.163), channel_id=1, source_target_pairs={{0,32},{2,34},{4,36},{6,38},{8,40},{10,42},{12,44},{14,46},{16,48}... | collective-permute-start | bytes 1572872 | tf_op jit(solution)/shard_map/ppermute | solution.py:11
  118.5 22.1 %collective-permute-start.12 = (f32[8,128,128]{2,1,0:T(8,128)S(1)}, f32[8,128,128]{2,1,0:T(8,128)S(1)}, u32[]{:S(2)}, u32[]{:S(2)}) collective-permute-start(f32[8,128,128]{2,1,0:T(8,128)S(1)} %add.184), channel_id=1, source_target_pairs={{0,64},{2,66},{4,68},{6,70},{8,72},{10,74},{12,76},{14,78},{16,80}... | collective-permute-start | bytes 1572872 | tf_op jit(solution)/shard_map/ppermute | solution.py:11
  137.3 0.8 copy-start.17
  139.0 39.1 %collective-permute-start.5 = (f32[8,128,128]{2,1,0:T(8,128)}, f32[8,128,128]{2,1,0:T(8,128)}, u32[]{:S(2)}, u32[]{:S(2)}) collective-permute-start(f32[8,128,128]{2,1,0:T(8,128)} %add.166), channel_id=1, source_target_pairs={{0,64},{2,66},{4,68},{6,70},{8,72},{10,74},{12,76},{14,78},{16,80}... | collective-permute-start | bytes 1572872 | tf_op jit(solution)/shard_map/ppermute | solution.py:11
  140.7 0.8 copy-start.19
  142.3 51.7 %collective-permute-start.13 = (f32[8,128,128]{2,1,0:T(8,128)}, f32[8,128,128]{2,1,0:T(8,128)}, u32[]{:S(2)}, u32[]{:S(2)}) collective-permute-start(f32[8,128,128]{2,1,0:T(8,128)} %add.186), channel_id=1, source_target_pairs={{0,128},{2,130},{4,132},{6,134},{8,136},{10,138},{12,140},{14,142}... | collective-permute-start | bytes 1572872 | tf_op jit(solution)/shard_map/ppermute | solution.py:11
  180.2 72.9 %collective-permute-start.6 = (f32[8,128,128]{2,1,0:T(8,128)}, f32[8,128,128]{2,1,0:T(8,128)}, u32[]{:S(2)}, u32[]{:S(2)}) collective-permute-start(f32[8,128,128]{2,1,0:T(8,128)} %add.169), channel_id=1, source_target_pairs={{0,128},{2,130},{4,132},{6,134},{8,136},{10,138},{12,140},{14,142}... | collective-permute-start | bytes 1572872 | tf_op jit(solution)/shard_map/ppermute | solution.py:11
  197.3 2.4 copy-start.6
  237.7 4.6 %copy-start.4 = (bf16[64,8,8,128]{3,2,1,0:T(8,128)(2,1)S(1)}, bf16[64,8,8,128]{3,2,1,0:T(8,128)(2,1)}, u32[]{:S(2)}) copy-start(bf16[64,8,8,128]{3,2,1,0:T(8,128)(2,1)} %copy-done.2) | copy-start | bytes 3145732
  251.1 2.0 copy-start.12
  251.1 2.0 copy-start.14
  251.6 1.4 copy-start.18
  253.1 2.2 copy-start.9
  255.3 1.2 copy-start.1
  255.3 1.9 copy-start.5
where the time goes:
time: 268 us; the launch traced here: 267 us
  waiting for transfers between devices  82.6 us (31%)
  starting transfers between devices  59.7 us (22%)
  blocking collectives  42.8 us (16%)
  local copies, waits for them, and re-layouts  35.1 us (13%)
  other arithmetic  26.1 us (10%)
  matrix products  19.9 us (7%)
    ppermute x14, waiting for transfers between devices, partner(): lax.ppermute(array, axis, [(i, i ^ 1 << distance) for i in range(lax.axis...  80.1 us
    ppermute x14, starting transfers between devices, partner(): lax.ppermute(array, axis, [(i, i ^ 1 << distance) for i in range(lax.axis...  40.6 us
    all_to_all x1, blocking collectives, body(): lax.all_to_all(value_part, 'head', split_axis=0, concat_axis=1, tiled=True)  33.7 us
    unnamed x53, local copies, waits for them, and re-layouts  14.1 us
    all_to_all x1, starting transfers between devices, body(): lax.all_to_all(out_grad, 'head', split_axis=1, concat_axis=0, tiled=True)  6.81 us
    add x6, other arithmetic, cross_states(): group_kv = group_kv + other_kv  6.39 us
    add x6, other arithmetic, cross_states(): group_qo = group_qo + other_qo  6.31 us
  transfers between devices with their start and end apart: 18, of which 12 were waited for; matrix products, arithmetic and copies ran while one was open for 23% of the time, Pallas kernels for 0%

commit v1 on v0

--- a/solution.py
+++ b/solution.py
@@ -2,6 +2,7 @@
 import jax.numpy as jnp
 from jax import lax
 from jax.sharding import PartitionSpec as P
+from jax.lax import all_to_all, axis_size
 
 DH = 128
 BLOCK = 128
@@ -149,7 +150,10 @@
     )
     return (
         lax.all_to_all(query_part, "head", split_axis=0, concat_axis=1, tiled=True),
-        lax.all_to_all(key_grad_part, "head", split_axis=0, concat_axis=1, tiled=True),
+        jnp.concatenate(
+            all_to_all(jnp.stack(jnp.split(key_grad_part, axis_size("head"), 0), 0), "head", 0, 0),
+            1,
+        ),
         lax.all_to_all(value_part, "head", split_axis=0, concat_axis=1, tiled=True),
     )
 

time: 268 us -> 268 us (level)
  blocking collectives: 42.8 us -> 9 us
  starting transfers between devices: 59.7 us -> 91.6 us
    all_to_all x2 -> x1, blocking collectives: 38.3 us -> 4.43 us  [body(): all_to_all(jnp.stack(jnp.split(key_grad_part, axis_size('head'), 0), 0),...]
    all_to_all x0 -> x1, starting transfers between devices: none -> 31.9 us  [body(): lax.all_to_all(value_part, 'head', split_axis=0, concat_axis=1, tiled=True)]
    unnamed x53 -> x55, local copies, waits for them, and re-layouts: 14.1 us -> 13.2 us
  transfers between devices with their start and end apart: 18 -> 19, of which waited for: 12 -> 12; matrix products, arithmetic and copies ran while one was open for 23% -> 23% of each run, Pallas kernels for 0% -> 0%
where the time goes in v1:
time: 268 us; the launch traced here: 267 us
  starting transfers between devices  91.6 us (34%)
  waiting for transfers between devices  82.6 us (31%)
  local copies, waits for them, and re-layouts  35.6 us (13%)
  other arithmetic  26.2 us (10%)
  matrix products  20.9 us (8%)
  blocking collectives  9 us (3%)
    ppermute x14, waiting for transfers between devices, partner(): lax.ppermute(array, axis, [(i, i ^ 1 << distance) for i in range(lax.axis...  80.1 us
    ppermute x14, starting transfers between devices, partner(): lax.ppermute(array, axis, [(i, i ^ 1 << distance) for i in range(lax.axis...  40.6 us
    all_to_all x1, starting transfers between devices, body(): lax.all_to_all(value_part, 'head', split_axis=0, concat_axis=1, tiled=True)  31.9 us
    unnamed x55, local copies, waits for them, and re-layouts  13.2 us
    all_to_all x1, starting transfers between devices, body(): lax.all_to_all(out_grad, 'head', split_axis=1, concat_axis=0, tiled=True)  6.81 us
    add x6, other arithmetic, cross_states(): group_kv = group_kv + other_kv  6.39 us
    add x6, other arithmetic, cross_states(): group_qo = group_qo + other_qo  6.31 us
  transfers between devices with their start and end apart: 19, of which 12 were waited for; matrix products, arithmetic and copies ran while one was open for 23% of the time, Pallas kernels for 0%

profile of v1, /device:TPU:1, one launch (start us, length us, event | category | flops | bytes accessed | tf_op | source)
XLA Modules:
  0.0 266.8 jit_solution(3276900026312689809)
XLA Ops:
  0.6 2.4 copy.183
  3.0 6.8 %all-to-all-start = ((bf16[256,2,1024]{2,0,1:T(8,128)(2,1)}), bf16[256,2,1024]{2,0,1:T(8,128)(2,1)S(1)}, u32[]{:S(2)}, u32[]{:S(2)}) async-start(bf16[256,2,1024]{2,0,1:T(8,128)(2,1)} %bitcast.98), calls=%async_computation | async-start | bytes 2097152 | tf_op jit(solution)/shard_map/all_to_all | solution.py:131
  9.8 1.1 copy.180
  11.6 3.9 %all-to-all-start.4 = ((bf16[256,2,1024]{2,0,1:T(8,128)(2,1)}), bf16[256,2,1024]{2,0,1:T(8,128)(2,1)S(1)}, u32[]{:S(2)}, u32[]{:S(2)}) async-start(bf16[256,2,1024]{2,0,1:T(8,128)(2,1)} %bitcast.95), calls=%async_computation.4 | async-start | bytes 2097152 | tf_op jit(solution)/shard_map/all_to_all | solution.py:128
  15.8 1.5 all-to-all-done.4
  17.5 2.7 %fusion.32 = (f32[8,128,128]{2,1,0:T(8,128)}, f32[4,8,128,128]{3,2,1,0:T(8,128)}) fusion(bf16[4,128,8,128]{3,2,1,0:T(8,128)(2,1)S(1)} %bitcast.103, bf16[4,128,8,128]{3,2,1,0:T(8,128)(2,1)S(1)} %bitcast.107), kind=kOutput, calls=%fused_computation.74 | convolution fusion | flops 134610944 | bytes 4718592 | tf_op jit(solution)/shard_map/nthd,nthe->nhde/dot_general | solution.py:72
  20.2 1.1 copy.181
  21.3 3.9 %all-to-all-start.2 = ((bf16[256,2,1024]{2,0,1:T(8,128)(2,1)}), bf16[256,2,1024]{2,0,1:T(8,128)(2,1)S(1)}, u32[]{:S(2)}, u32[]{:S(2)}) async-start(bf16[256,2,1024]{2,0,1:T(8,128)(2,1)} %bitcast.121), calls=%async_computation.2 | async-start | bytes 2097152 | tf_op jit(solution)/shard_map/all_to_all | solution.py:129
  25.2 2.3 copy.182
  27.5 4.4 %all-to-all-start.1 = ((bf16[256,2,1024]{2,0,1:T(8,128)(2,1)}), bf16[256,2,1024]{2,0,1:T(8,128)(2,1)}, u32[]{:S(2)}, u32[]{:S(2)}) async-start(bf16[256,2,1024]{2,0,1:T(8,128)(2,1)} %bitcast.120), calls=%async_computation.1 | async-start | bytes 2097152 | tf_op jit(solution)/shard_map/all_to_all | solution.py:130
  32.0 1.5 copy.136
  33.8 1.5 copy.135
  35.3 2.6 fusion.31
  38.0 1.7 collective-permute-start
  39.7 2.0 add.176
  41.8 1.0 collective-permute-start.8
  42.8 1.5 slice_reduce_fusion
  44.3 7.7 %collective-permute-done = f32[8,128,128]{2,1,0:T(8,128)} collective-permute-done((f32[8,128,128]{2,1,0:T(8,128)}, f32[8,128,128]{2,1,0:T(8,128)}, u32[]{:S(2)}, u32[]{:S(2)}) %collective-permute-start) | collective-permute-done | bytes 524320 | tf_op jit(solution)/shard_map/ppermute | solution.py:12
  52.0 1.3 add.154
  53.3 1.7 collective-permute-start.1
  55.0 9.0 %collective-permute-done.8 = f32[8,128,128]{2,1,0:T(8,128)} collective-permute-done((f32[8,128,128]{2,1,0:T(8,128)}, f32[8,128,128]{2,1,0:T(8,128)}, u32[]{:S(2)}, u32[]{:S(2)}) %collective-permute-start.8) | collective-permute-done | bytes 524320 | tf_op jit(solution)/shard_map/ppermute | solution.py:12
  63.9 1.3 add.178
  65.2 1.4 collective-permute-start.9
  67.2 7.9 %collective-permute-done.1 = f32[8,128,128]{2,1,0:T(8,128)S(1)} collective-permute-done((f32[8,128,128]{2,1,0:T(8,128)S(1)}, f32[8,128,128]{2,1,0:T(8,128)S(1)}, u32[]{:S(2)}, u32[]{:S(2)}) %collective-permute-start.1) | collective-permute-done | bytes 524320 | tf_op jit(solution)/shard_map/ppermute | solution.py:12
  75.2 1.4 collective-permute-start.2
  76.8 3.0 %collective-permute-start.10 = (f32[8,128,128]{2,1,0:T(8,128)S(1)}, f32[8,128,128]{2,1,0:T(8,128)S(1)}, u32[]{:S(2)}, u32[]{:S(2)}) collective-permute-start(f32[8,128,128]{2,1,0:T(8,128)S(1)} %add.180), channel_id=1, source_target_pairs={{0,16},{2,18},{4,20},{6,22},{8,24},{10,26},{12,28},{14,30},{16,0},... | collective-permute-start | bytes 1572872 | tf_op jit(solution)/shard_map/ppermute | solution.py:12
  80.1 1.1 pad_bitcast_fusion
  81.2 1.2 fusion.4
  82.4 6.9 %collective-permute-done.2 = f32[8,128,128]{2,1,0:T(8,128)S(1)} collective-permute-done((f32[8,128,128]{2,1,0:T(8,128)S(1)}, f32[8,128,128]{2,1,0:T(8,128)S(1)}, u32[]{:S(2)}, u32[]{:S(2)}) %collective-permute-start.2) | collective-permute-done | bytes 524320 | tf_op jit(solution)/shard_map/ppermute | solution.py:12
  91.0 2.9 %collective-permute-start.3 = (f32[8,128,128]{2,1,0:T(8,128)}, f32[8,128,128]{2,1,0:T(8,128)}, u32[]{:S(2)}, u32[]{:S(2)}) collective-permute-start(f32[8,128,128]{2,1,0:T(8,128)} %add.160), channel_id=1, source_target_pairs={{0,16},{2,18},{4,20},{6,22},{8,24},{10,26},{12,28},{14,30},{16,0},... | collective-permute-start | bytes 1572872 | tf_op jit(solution)/shard_map/ppermute | solution.py:12
  93.9 9.1 %collective-permute-done.10 = f32[8,128,128]{2,1,0:T(8,128)S(1)} collective-permute-done((f32[8,128,128]{2,1,0:T(8,128)S(1)}, f32[8,128,128]{2,1,0:T(8,128)S(1)}, u32[]{:S(2)}, u32[]{:S(2)}) %collective-permute-start.10) | collective-permute-done | bytes 524320 | tf_op jit(solution)/shard_map/ppermute | solution.py:12
  104.6 1.6 collective-permute-start.11
  106.2 1.5 pad_add_fusion
  107.7 2.9 %copy.104 = f32[2,2,8,128,128]{3,4,2,1,0:T(8,128)} copy(f32[2,2,8,128,128]{4,3,2,0,1:T(8,128)} %pad_add_fusion) | data formatting | bytes 4194304 | tf_op jit(solution)/shard_map/add | solution.py:33
  110.7 1.7 pad_add_fusion.1
  112.4 1.5 copy.93
  114.3 1.3 add.163
  115.6 1.7 collective-permute-start.4
  117.3 1.3 add.184
  118.5 3.2 %collective-permute-start.12 = (f32[8,128,128]{2,1,0:T(8,128)S(1)}, f32[8,128,128]{2,1,0:T(8,128)S(1)}, u32[]{:S(2)}, u32[]{:S(2)}) collective-permute-start(f32[8,128,128]{2,1,0:T(8,128)S(1)} %add.184), channel_id=1, source_target_pairs={{0,64},{2,66},{4,68},{6,70},{8,72},{10,74},{12,76},{14,78},{16,80}... | collective-permute-start | bytes 1572872 | tf_op jit(solution)/shard_map/ppermute | solution.py:12
  122.7 1.9 fusion.12
  124.5 12.8 %collective-permute-done.4 = f32[8,128,128]{2,1,0:T(8,128)S(1)} collective-permute-done((f32[8,128,128]{2,1,0:T(8,128)S(1)}, f32[8,128,128]{2,1,0:T(8,128)S(1)}, u32[]{:S(2)}, u32[]{:S(2)}) %collective-permute-start.4) | collective-permute-done | bytes 524320 | tf_op jit(solution)/shard_map/ppermute | solution.py:12
  139.0 1.7 collective-permute-start.5
  142.3 5.3 %collective-permute-start.13 = (f32[8,128,128]{2,1,0:T(8,128)}, f32[8,128,128]{2,1,0:T(8,128)}, u32[]{:S(2)}, u32[]{:S(2)}) collective-permute-start(f32[8,128,128]{2,1,0:T(8,128)} %add.186), channel_id=1, source_target_pairs={{0,128},{2,130},{4,132},{6,134},{8,136},{10,138},{12,140},{14,142}... | collective-permute-start | bytes 1572872 | tf_op jit(solution)/shard_map/ppermute | solution.py:12
  147.7 1.7 fusion.22
  149.4 2.6 fusion.3
  151.9 26.1 %collective-permute-done.5 = f32[8,128,128]{2,1,0:T(8,128)} collective-permute-done((f32[8,128,128]{2,1,0:T(8,128)}, f32[8,128,128]{2,1,0:T(8,128)}, u32[]{:S(2)}, u32[]{:S(2)}) %collective-permute-start.5) | collective-permute-done | bytes 524320 | tf_op jit(solution)/shard_map/ppermute | solution.py:12
  178.1 2.1 add.169
  180.2 13.8 %collective-permute-start.6 = (f32[8,128,128]{2,1,0:T(8,128)}, f32[8,128,128]{2,1,0:T(8,128)}, u32[]{:S(2)}, u32[]{:S(2)}) collective-permute-start(f32[8,128,128]{2,1,0:T(8,128)} %add.169), channel_id=1, source_target_pairs={{0,128},{2,130},{4,132},{6,134},{8,136},{10,138},{12,140},{14,142}... | collective-permute-start | bytes 1572872 | tf_op jit(solution)/shard_map/ppermute | solution.py:12
  194.0 2.3 multiply_add_fusion
  197.3 2.1 bitcast_add_fusion.2
  199.7 2.3 fusion
  202.0 1.7 copy.118
  203.7 2.4 all_to_all.96
  206.1 31.9 %all-to-all-start.6 = ((bf16[2,256,1024]{2,1,0:T(8,128)(2,1)}), bf16[2,256,1024]{2,1,0:T(8,128)(2,1)}, u32[]{:S(2)}, u32[]{:S(2)}) async-start(bf16[2,256,1024]{2,1,0:T(8,128)(2,1)} %all_to_all.96), calls=%async_computation.6 | async-start | bytes 2097152 | tf_op jit(solution)/shard_map/all_to_all | solution.py:157
  237.9 3.9 %fusion.1 = bf16[4,128,8,128]{3,1,2,0:T(8,128)(2,1)} fusion(f32[4,8,128,128]{3,2,1,0:T(8,128)} %fusion.12, f32[4,8,128,128]{2,3,1,0:T(8,128)S(1)} %bitcast_add_fusion.2, bf16[4,128,8,128]{3,2,1,0:T(8,128)(2,1)S(1)} %bitcast.112), kind=kOutput, calls=%fused_computation.3 | convolution fusion | flops 806354944 | bytes 6291456 | tf_op jit(solution)/shard_map/nshe,nhde->nshd/dot_general | solution.py:106
  241.9 1.6 copy.119
  243.4 1.4 copy.122
  246.2 4.4 %all_to_all.107 = bf16[2,256,1024]{2,1,0:T(8,128)(2,1)S(1)} all-to-all(bf16[2,256,1024]{2,1,0:T(8,128)(2,1)S(1)} %pad_maximum_fusion), channel_id=1, replica_groups=mesh['seq'=128,'head'=2] {'head'}, dimensions={0} | all-to-all | bytes 2097152 | tf_op jit(solution)/shard_map/all_to_all | solution.py:154
  251.2 1.4 copy.121
  252.7 2.0 multiply_add_fusion.1
  256.8 2.3 fusion.2
  260.3 4.6 %all_to_all.108 = bf16[2,256,1024]{2,1,0:T(8,128)(2,1)S(1)} all-to-all(bf16[2,256,1024]{2,1,0:T(8,128)(2,1)S(1)} %all_to_all.88), channel_id=1, replica_groups=mesh['seq'=128,'head'=2] {'head'}, dimensions={0} | all-to-all | bytes 2097152 | tf_op jit(solution)/shard_map/all_to_all | solution.py:152
  265.4 1.4 copy.120
  (88 shorter events, 17.6 us)
Async XLA Ops:
  0.6 9.2 %copy-start.21 = (bf16[256,2048]{1,0:T(8,128)(2,1)S(1)}, bf16[256,2048]{1,0:T(8,128)(2,1)}, u32[]{:S(2)}) copy-start(bf16[256,2048]{1,0:T(8,128)(2,1)} %param.5) | copy-start | bytes 3145732
  3.0 8.6 %all-to-all-start = ((bf16[256,2,1024]{2,0,1:T(8,128)(2,1)}), bf16[256,2,1024]{2,0,1:T(8,128)(2,1)S(1)}, u32[]{:S(2)}, u32[]{:S(2)}) async-start(bf16[256,2,1024]{2,0,1:T(8,128)(2,1)} %bitcast.98), calls=%async_computation | async-start | bytes 2097152 | tf_op jit(solution)/shard_map/all_to_all | solution.py:131
  11.6 5.7 %all-to-all-start.4 = ((bf16[256,2,1024]{2,0,1:T(8,128)(2,1)}), bf16[256,2,1024]{2,0,1:T(8,128)(2,1)S(1)}, u32[]{:S(2)}, u32[]{:S(2)}) async-start(bf16[256,2,1024]{2,0,1:T(8,128)(2,1)} %bitcast.95), calls=%async_computation.4 | async-start | bytes 2097152 | tf_op jit(solution)/shard_map/all_to_all | solution.py:128
  15.8 133.6 %copy-start = (bf16[64,8,8,128]{3,2,1,0:T(8,128)(2,1)}, bf16[64,8,8,128]{3,2,1,0:T(8,128)(2,1)S(1)}, u32[]{:S(2)}) copy-start(bf16[64,8,8,128]{3,2,1,0:T(8,128)(2,1)S(1)} %copy.134) | copy-start | bytes 3145732
  17.5 2.7 %copy-start.22 = (bf16[256,2048]{1,0:T(8,128)(2,1)S(1)}, bf16[256,2048]{1,0:T(8,128)(2,1)}, u32[]{:S(2)}) copy-start(bf16[256,2048]{1,0:T(8,128)(2,1)} %param.6) | copy-start | bytes 3145732
  20.2 19.5 %collective-permute-start.7 = (f32[8,128,128]{2,1,0:T(8,128)}, f32[8,128,128]{2,1,0:T(8,128)}, u32[]{:S(2)}, u32[]{:S(2)}) collective-permute-start(f32[8,128,128]{2,1,0:T(8,128)} %get-tuple-element.34), channel_id=1, source_target_pairs={{0,2},{2,0},{4,6},{6,4},{8,10},{10,8},{12,14},{14,12},{16,18},{18,... | collective-permute-start | bytes 1572872 | tf_op jit(solution)/shard_map/ppermute | solution.py:12
  21.3 6.2 %all-to-all-start.2 = ((bf16[256,2,1024]{2,0,1:T(8,128)(2,1)}), bf16[256,2,1024]{2,0,1:T(8,128)(2,1)S(1)}, u32[]{:S(2)}, u32[]{:S(2)}) async-start(bf16[256,2,1024]{2,0,1:T(8,128)(2,1)} %bitcast.121), calls=%async_computation.2 | async-start | bytes 2097152 | tf_op jit(solution)/shard_map/all_to_all | solution.py:129
  27.5 4.4 %copy-start.10 = (bf16[256,2,1024]{2,0,1:T(8,128)(2,1)}, bf16[256,2,1024]{2,0,1:T(8,128)(2,1)S(1)}, u32[]{:S(2)}) copy-start(bf16[256,2,1024]{2,0,1:T(8,128)(2,1)S(1)} %all-to-all-done.2) | copy-start | bytes 3145732
  27.5 6.3 %all-to-all-start.1 = ((bf16[256,2,1024]{2,0,1:T(8,128)(2,1)}), bf16[256,2,1024]{2,0,1:T(8,128)(2,1)}, u32[]{:S(2)}, u32[]{:S(2)}) async-start(bf16[256,2,1024]{2,0,1:T(8,128)(2,1)} %bitcast.120), calls=%async_computation.1 | async-start | bytes 2097152 | tf_op jit(solution)/shard_map/all_to_all | solution.py:130
  35.3 2.7 copy-start.2
  38.0 6.3 %copy-start.23 = (f32[16,11]{1,0:T(8,128)S(1)}, f32[16,11]{1,0:T(8,128)}, u32[]{:S(2)}) copy-start(f32[16,11]{1,0:T(8,128)} %param.9) | copy-start | bytes 2116
  38.0 14.1 %collective-permute-start = (f32[8,128,128]{2,1,0:T(8,128)}, f32[8,128,128]{2,1,0:T(8,128)}, u32[]{:S(2)}, u32[]{:S(2)}) collective-permute-start(f32[8,128,128]{2,1,0:T(8,128)} %get-tuple-element.32), channel_id=1, source_target_pairs={{0,2},{2,0},{4,6},{6,4},{8,10},{10,8},{12,14},{14,12},{16,18},{18,... | collective-permute-start | bytes 1572872 | tf_op jit(solution)/shard_map/ppermute | solution.py:12
  41.8 22.2 %collective-permute-start.8 = (f32[8,128,128]{2,1,0:T(8,128)}, f32[8,128,128]{2,1,0:T(8,128)}, u32[]{:S(2)}, u32[]{:S(2)}) collective-permute-start(f32[8,128,128]{2,1,0:T(8,128)} %add.176), channel_id=1, source_target_pairs={{0,4},{2,6},{4,0},{6,2},{8,12},{10,14},{12,8},{14,10},{16,20},{18,... | collective-permute-start | bytes 1572872 | tf_op jit(solution)/shard_map/ppermute | solution.py:12
  42.8 24.1 %copy-start.8 = (f32[4,8,128,128]{3,2,1,0:T(8,128)S(1)}, f32[4,8,128,128]{3,2,1,0:T(8,128)}, u32[]{:S(2)}) copy-start(f32[4,8,128,128]{3,2,1,0:T(8,128)} %get-tuple-element.33) | copy-start | bytes 6291460
  53.3 21.8 %collective-permute-start.1 = (f32[8,128,128]{2,1,0:T(8,128)S(1)}, f32[8,128,128]{2,1,0:T(8,128)S(1)}, u32[]{:S(2)}, u32[]{:S(2)}) collective-permute-start(f32[8,128,128]{2,1,0:T(8,128)S(1)} %add.154), channel_id=1, source_target_pairs={{0,4},{2,6},{4,0},{6,2},{8,12},{10,14},{12,8},{14,10},{16,20},{18,... | collective-permute-start | bytes 1572872 | tf_op jit(solution)/shard_map/ppermute | solution.py:12
  65.2 11.5 %collective-permute-start.9 = (f32[8,128,128]{2,1,0:T(8,128)S(1)}, f32[8,128,128]{2,1,0:T(8,128)S(1)}, u32[]{:S(2)}, u32[]{:S(2)}) collective-permute-start(f32[8,128,128]{2,1,0:T(8,128)S(1)} %add.178), channel_id=1, source_target_pairs={{0,8},{2,10},{4,12},{6,14},{8,0},{10,2},{12,4},{14,6},{16,24},{18,... | collective-permute-start | bytes 1572872 | tf_op jit(solution)/shard_map/ppermute | solution.py:12
  75.1 6.1 %copy-start.12 = (f32[8,128,128]{2,1,0:T(8,128)}, f32[8,128,128]{2,1,0:T(8,128)S(1)}, u32[]{:S(2)}) copy-start(f32[8,128,128]{2,1,0:T(8,128)S(1)} %collective-permute-done.1) | copy-start | bytes 1572868
  75.2 6.0 %copy-start.7 = (f32[4,8,128,128]{3,2,1,0:T(8,128)S(1)}, f32[4,8,128,128]{3,2,1,0:T(8,128)}, u32[]{:S(2)}) copy-start(f32[4,8,128,128]{3,2,1,0:T(8,128)} %get-tuple-element.35) | copy-start | bytes 6291460
  75.2 14.1 %collective-permute-start.2 = (f32[8,128,128]{2,1,0:T(8,128)S(1)}, f32[8,128,128]{2,1,0:T(8,128)S(1)}, u32[]{:S(2)}, u32[]{:S(2)}) collective-permute-start(f32[8,128,128]{2,1,0:T(8,128)S(1)} %add.157), channel_id=1, source_target_pairs={{0,8},{2,10},{4,12},{6,14},{8,0},{10,2},{12,4},{14,6},{16,24},{18,... | collective-permute-start | bytes 1572872 | tf_op jit(solution)/shard_map/ppermute | solution.py:12
  76.7 3.4 %copy-start.16 = (f32[8,128,128]{2,1,0:T(8,128)}, f32[8,128,128]{2,1,0:T(8,128)S(1)}, u32[]{:S(2)}) copy-start(f32[8,128,128]{2,1,0:T(8,128)S(1)} %collective-permute-done.9) | copy-start | bytes 1572868
  76.8 26.2 %collective-permute-start.10 = (f32[8,128,128]{2,1,0:T(8,128)S(1)}, f32[8,128,128]{2,1,0:T(8,128)S(1)}, u32[]{:S(2)}, u32[]{:S(2)}) collective-permute-start(f32[8,128,128]{2,1,0:T(8,128)S(1)} %add.180), channel_id=1, source_target_pairs={{0,16},{2,18},{4,20},{6,22},{8,24},{10,26},{12,28},{14,30},{16,0},... | collective-permute-start | bytes 1572872 | tf_op jit(solution)/shard_map/ppermute | solution.py:12
  89.3 0.8 copy-start.14
  91.0 23.3 %collective-permute-start.3 = (f32[8,128,128]{2,1,0:T(8,128)}, f32[8,128,128]{2,1,0:T(8,128)}, u32[]{:S(2)}, u32[]{:S(2)}) collective-permute-start(f32[8,128,128]{2,1,0:T(8,128)} %add.160), channel_id=1, source_target_pairs={{0,16},{2,18},{4,20},{6,22},{8,24},{10,26},{12,28},{14,30},{16,0},... | collective-permute-start | bytes 1572872 | tf_op jit(solution)/shard_map/ppermute | solution.py:12
  103.0 0.8 copy-start.19
  104.6 12.7 %collective-permute-start.11 = (f32[8,128,128]{2,1,0:T(8,128)}, f32[8,128,128]{2,1,0:T(8,128)}, u32[]{:S(2)}, u32[]{:S(2)}) collective-permute-start(f32[8,128,128]{2,1,0:T(8,128)} %add.182), channel_id=1, source_target_pairs={{0,32},{2,34},{4,36},{6,38},{8,40},{10,42},{12,44},{14,46},{16,48}... | collective-permute-start | bytes 1572872 | tf_op jit(solution)/shard_map/ppermute | solution.py:12
  113.9 7.9 %copy-start.3 = (bf16[64,8,8,128]{3,2,1,0:T(8,128)(2,1)S(1)}, bf16[64,8,8,128]{3,2,1,0:T(8,128)(2,1)}, u32[]{:S(2)}) copy-start(bf16[64,8,8,128]{3,2,1,0:T(8,128)(2,1)} %copy-done.2) | copy-start | bytes 3145732
  115.6 21.8 %collective-permute-start.4 = (f32[8,128,128]{2,1,0:T(8,128)S(1)}, f32[8,128,128]{2,1,0:T(8,128)S(1)}, u32[]{:S(2)}, u32[]{:S(2)}) collective-permute-start(f32[8,128,128]{2,1,0:T(8,128)S(1)} %add.163), channel_id=1, source_target_pairs={{0,32},{2,34},{4,36},{6,38},{8,40},{10,42},{12,44},{14,46},{16,48}... | collective-permute-start | bytes 1572872 | tf_op jit(solution)/shard_map/ppermute | solution.py:12
  118.5 22.1 %collective-permute-start.12 = (f32[8,128,128]{2,1,0:T(8,128)S(1)}, f32[8,128,128]{2,1,0:T(8,128)S(1)}, u32[]{:S(2)}, u32[]{:S(2)}) collective-permute-start(f32[8,128,128]{2,1,0:T(8,128)S(1)} %add.184), channel_id=1, source_target_pairs={{0,64},{2,66},{4,68},{6,70},{8,72},{10,74},{12,76},{14,78},{16,80}... | collective-permute-start | bytes 1572872 | tf_op jit(solution)/shard_map/ppermute | solution.py:12
  137.3 0.8 copy-start.17
  139.0 39.1 %collective-permute-start.5 = (f32[8,128,128]{2,1,0:T(8,128)}, f32[8,128,128]{2,1,0:T(8,128)}, u32[]{:S(2)}, u32[]{:S(2)}) collective-permute-start(f32[8,128,128]{2,1,0:T(8,128)} %add.166), channel_id=1, source_target_pairs={{0,64},{2,66},{4,68},{6,70},{8,72},{10,74},{12,76},{14,78},{16,80}... | collective-permute-start | bytes 1572872 | tf_op jit(solution)/shard_map/ppermute | solution.py:12
  140.7 0.8 copy-start.20
  142.3 51.7 %collective-permute-start.13 = (f32[8,128,128]{2,1,0:T(8,128)}, f32[8,128,128]{2,1,0:T(8,128)}, u32[]{:S(2)}, u32[]{:S(2)}) collective-permute-start(f32[8,128,128]{2,1,0:T(8,128)} %add.186), channel_id=1, source_target_pairs={{0,128},{2,130},{4,132},{6,134},{8,136},{10,138},{12,140},{14,142}... | collective-permute-start | bytes 1572872 | tf_op jit(solution)/shard_map/ppermute | solution.py:12
  180.2 72.5 %collective-permute-start.6 = (f32[8,128,128]{2,1,0:T(8,128)}, f32[8,128,128]{2,1,0:T(8,128)}, u32[]{:S(2)}, u32[]{:S(2)}) collective-permute-start(f32[8,128,128]{2,1,0:T(8,128)} %add.169), channel_id=1, source_target_pairs={{0,128},{2,130},{4,132},{6,134},{8,136},{10,138},{12,140},{14,142}... | collective-permute-start | bytes 1572872 | tf_op jit(solution)/shard_map/ppermute | solution.py:12
  197.3 2.4 copy-start.6
  203.7 34.2 %copy-start.4 = (bf16[64,8,8,128]{3,2,1,0:T(8,128)(2,1)S(1)}, bf16[64,8,8,128]{3,2,1,0:T(8,128)(2,1)}, u32[]{:S(2)}) copy-start(bf16[64,8,8,128]{3,2,1,0:T(8,128)(2,1)} %copy-done.2) | copy-start | bytes 3145732
  206.1 35.8 %all-to-all-start.6 = ((bf16[2,256,1024]{2,1,0:T(8,128)(2,1)}), bf16[2,256,1024]{2,1,0:T(8,128)(2,1)}, u32[]{:S(2)}, u32[]{:S(2)}) async-start(bf16[2,256,1024]{2,1,0:T(8,128)(2,1)} %all_to_all.96), calls=%async_computation.6 | async-start | bytes 2097152 | tf_op jit(solution)/shard_map/all_to_all | solution.py:157
  241.8 3.0 %copy-start.11 = (bf16[4,128,8,128]{3,1,2,0:T(8,128)(2,1)S(1)}, bf16[4,128,8,128]{3,1,2,0:T(8,128)(2,1)}, u32[]{:S(2)}) copy-start(bf16[4,128,8,128]{3,1,2,0:T(8,128)(2,1)} %fusion.1) | copy-start | bytes 3145732
  250.7 2.0 copy-start.13
  250.7 2.0 copy-start.15
  251.2 1.4 copy-start.18
  252.6 2.2 copy-start.9
  254.9 1.2 copy-start.1
  254.9 1.9 copy-start.5
